TPU v7x, 32 devices: a whole 2x2x4 slice. The times are simulated.
32 devices in a mesh: dp: 8 (over z, core), tensor: 4 (over y, x).
Axes of the slice: x: 2, y: 2, z: 4, core: 2. Of those that a mesh axis runs over, the one named last changes fastest.
Arguments:
- inputs: bfloat16 [49152, 512], P(('dp', 'tensor')), may hold values from -6 to 6
- w_qkv: bfloat16 [2, 3, 512, 512], P(None, None, 'dp', 'tensor'), may hold values from -0.25 to 0.25
- w_out: bfloat16 [2, 512, 512], P(None, 'tensor', 'dp'), may hold values from -0.75 to 0.75
- w_up: bfloat16 [2, 512, 2048], P(None, 'dp', 'tensor'), may hold values from -0.25 to 0.25
- w_down: bfloat16 [2, 2048, 512], P(None, 'tensor', 'dp'), may hold values from -0.125 to 0.125
- ln_gain: float32 [2, 2, 512], replicated, may hold values from 0.5 to 1.5
- ln_bias: float32 [2, 2, 512], replicated, may hold values from -3 to 3
- bias_qv: float32 [2, 2, 512], P(None, None, 'tensor'), may hold values from -3 to 3
- bias_up: float32 [2, 2048], P(None, 'tensor'), may hold values from -3 to 3
- branch_bias: float32 [2, 2, 512], replicated, may hold values from -3 to 3
- cotangent: float32 [49152, 512], P(('dp', 'tensor')), may hold values from -6 to 6
Outputs:
- outputs: bfloat16 [49152, 512], P(('dp', 'tensor'))
- input_grad: float32 [49152, 512], P(('dp', 'tensor'))
- grad_qkv: float32 [2, 3, 512, 512], P(None, None, 'dp', 'tensor')
- grad_out: float32 [2, 512, 512], P(None, 'tensor', 'dp')
- grad_up: float32 [2, 512, 2048], P(None, 'dp', 'tensor')
- grad_down: float32 [2, 2048, 512], P(None, 'tensor', 'dp')
- grad_ln_gain: float32 [2, 2, 512], replicated
- grad_ln_bias: float32 [2, 2, 512], replicated
- grad_bias_qv: float32 [2, 2, 512], P(None, None, 'tensor')
- grad_bias_up: float32 [2, 2048], P(None, 'tensor')
- grad_branch_bias: float32 [2, 2, 512], replicated
All inputs are finite; a program needn't handle non-finite values.
Results may differ from a plain program's by a relative error of at most 0.025.
Values may be sent and summed in bfloat16 or wider, within the bound.
A program may use at most 320 MiB of HBM per device.

v0:
```python
import math
import jax
import jax.numpy as jnp
from jax import lax
from jax.sharding import PartitionSpec as P

HD = 64
SPAN = 128
LEN = 2048
LAYERS = 2
highest = lax.Precision.HIGHEST
epsilon = 1e-05
masked_score = -1e30


def normalize(rows, gain, shift):
    centre = rows - jnp.mean(rows, -1, keepdims=True)
    spread = jnp.mean(centre * centre, -1, keepdims=True)
    return centre * lax.rsqrt(spread + epsilon) * gain + shift


def gelu_exact(values):
    return jax.nn.gelu(values, approximate=False)


def to_heads(rows):
    return rows.reshape(-1, LEN // SPAN, SPAN, rows.shape[1] // HD, HD)


def score_blocks(head_queries, head_keys, key_mean):
    scale = HD ** (-0.5)
    blocks = LEN // SPAN
    direct = (
        jnp.einsum(
            "gbihe,gbjhe->gbhij", head_queries, head_keys, preferred_element_type=jnp.float32
        )
        * scale
    )
    summary = jnp.einsum(
        "gbihe,gche->gbhic", head_queries.astype(jnp.float32), key_mean, precision=highest
    ) * scale + math.log(SPAN)
    inside = lax.broadcasted_iota(jnp.int32, (SPAN, SPAN), 0) >= lax.broadcasted_iota(
        jnp.int32, (SPAN, SPAN), 1
    )
    earlier = lax.broadcasted_iota(jnp.int32, (blocks, 1, 1, blocks), 0) > lax.broadcasted_iota(
        jnp.int32, (blocks, 1, 1, blocks), 3
    )
    return (jnp.where(inside, direct, masked_score), jnp.where(earlier, summary, masked_score))


def attend(query_rows, key_rows, value_rows):
    head_queries, head_keys, head_values = (
        to_heads(query_rows),
        to_heads(key_rows),
        to_heads(value_rows),
    )
    key_mean = jnp.mean(head_keys.astype(jnp.float32), 2)
    value_mean = jnp.mean(head_values.astype(jnp.float32), 2)
    direct, summary = score_blocks(head_queries, head_keys, key_mean)
    top = jnp.maximum(jnp.max(direct, -1), jnp.max(summary, -1))[..., None]
    direct_weight = jnp.exp(direct - top)
    summary_weight = jnp.exp(summary - top)
    total = jnp.sum(direct_weight, -1, keepdims=True) + jnp.sum(summary_weight, -1, keepdims=True)
    direct_prob = direct_weight / total
    summary_prob = summary_weight / total
    mixed = jnp.einsum(
        "gbhij,gbjhe->gbihe",
        direct_prob.astype(jnp.bfloat16),
        head_values,
        preferred_element_type=jnp.float32,
    )
    mixed = mixed + jnp.einsum("gbhic,gche->gbihe", summary_prob, value_mean, precision=highest)
    log_total = (top + jnp.log(total))[..., 0]
    return (mixed.reshape(query_rows.shape), log_total)


def attend_back(query_rows, key_rows, value_rows, log_total, grad_rows):
    scale = HD ** (-0.5)
    head_queries, head_keys, head_values = (
        to_heads(query_rows),
        to_heads(key_rows),
        to_heads(value_rows),
    )
    head_grads = to_heads(grad_rows)
    key_mean = jnp.mean(head_keys.astype(jnp.float32), 2)
    value_mean = jnp.mean(head_values.astype(jnp.float32), 2)
    direct, summary = score_blocks(head_queries, head_keys, key_mean)
    direct_prob = jnp.exp(direct - log_total[..., None])
    summary_prob = jnp.exp(summary - log_total[..., None])
    grad_float = head_grads.astype(jnp.float32)
    query_float = head_queries.astype(jnp.float32)
    direct_grad = jnp.einsum(
        "gbihe,gbjhe->gbhij", head_grads, head_values, preferred_element_type=jnp.float32
    )
    summary_grad = jnp.einsum("gbihe,gche->gbhic", grad_float, value_mean, precision=highest)
    centre = jnp.sum(direct_prob * direct_grad, -1, keepdims=True) + jnp.sum(
        summary_prob * summary_grad, -1, keepdims=True
    )
    direct_score = (direct_prob * (direct_grad - centre)).astype(jnp.bfloat16)
    summary_score = summary_prob * (summary_grad - centre)
    grad_query = jnp.einsum(
        "gbhij,gbjhe->gbihe", direct_score, head_keys, preferred_element_type=jnp.float32
    )
    grad_query = (
        grad_query + jnp.einsum("gbhic,gche->gbihe", summary_score, key_mean, precision=highest)
    ) * scale
    key_block = jnp.einsum("gbhic,gbihe->gche", summary_score, query_float, precision=highest) * (
        scale / SPAN
    )
    grad_key = (
        jnp.einsum(
            "gbhij,gbihe->gbjhe", direct_score, head_queries, preferred_element_type=jnp.float32
        )
        * scale
        + key_block[:, :, None]
    )
    value_block = (
        jnp.einsum("gbhic,gbihe->gche", summary_prob, grad_float, precision=highest) / SPAN
    )
    grad_value = (
        jnp.einsum(
            "gbhij,gbihe->gbjhe",
            direct_prob.astype(jnp.bfloat16),
            head_grads,
            preferred_element_type=jnp.float32,
        )
        + value_block[:, :, None]
    )
    shape = query_rows.shape
    return (grad_query.reshape(shape), grad_key.reshape(shape), grad_value.reshape(shape))


def fetch(first, second, third, fourth):
    return (
        lax.all_gather(first, "dp", axis=2, tiled=True),
        lax.all_gather(second, "dp", axis=2, tiled=True),
        lax.all_gather(third, "dp", axis=1, tiled=True),
        lax.all_gather(fourth, "dp", axis=2, tiled=True),
    )


def return_grads(first, second, third, fourth):
    return (
        lax.psum_scatter(first.astype(jnp.bfloat16), "dp", scatter_dimension=2, tiled=True).astype(
            jnp.float32
        ),
        lax.psum_scatter(second.astype(jnp.bfloat16), "dp", scatter_dimension=2, tiled=True).astype(
            jnp.float32
        ),
        lax.psum_scatter(third.astype(jnp.bfloat16), "dp", scatter_dimension=1, tiled=True).astype(
            jnp.float32
        ),
        lax.psum_scatter(fourth.astype(jnp.bfloat16), "dp", scatter_dimension=2, tiled=True).astype(
            jnp.float32
        ),
    )


def layer_weights(w_qkv, w_out, w_up, w_down, layer):
    gathered = fetch(
        w_qkv[layer : layer + 1],
        w_out[layer : layer + 1],
        w_up[layer : layer + 1],
        w_down[layer : layer + 1],
    )
    return tuple((part[0] for part in gathered))


def spread_only(rows, project):
    return project(lax.all_gather(rows, "tensor", axis=0, tiled=True))


def fold_again(rows, grads):
    return jnp.einsum(
        "td,tc->dc",
        lax.all_gather(rows, "tensor", axis=0, tiled=True),
        grads,
        preferred_element_type=jnp.float32,
    )


def spread_grads(rows, project):
    piece = lax.all_gather(rows, "tensor", axis=0, tiled=True)
    return (piece, project(piece))


def slice_term(source, weight, form):
    return jnp.einsum(form, source, weight, preferred_element_type=jnp.float32)


def rows_sum(source, weight, form):
    return lax.psum_scatter(
        slice_term(source, weight, form).astype(jnp.bfloat16),
        "tensor",
        scatter_dimension=0,
        tiled=True,
    ).astype(jnp.float32)


def grads_sum(source, weight, form):
    return lax.psum_scatter(
        slice_term(source, weight, form).astype(jnp.bfloat16),
        "tensor",
        scatter_dimension=0,
        tiled=True,
    ).astype(jnp.float32)


def group_rows(token_att, out_whole):
    groups = lax.axis_size("tensor")
    parts = token_att.reshape(token_att.shape[0], groups, -1)
    grouped = out_whole.reshape(groups, -1, out_whole.shape[1])
    partial_value = jnp.einsum("tgc,gcd->tgd", parts, grouped, preferred_element_type=jnp.float32)
    return jnp.sum(partial_value.astype(jnp.bfloat16), 1, dtype=jnp.float32)


def group_grads(token_grads, qkv_whole):
    groups = lax.axis_size("tensor")
    parts = token_grads.reshape(token_grads.shape[0], 3, groups, -1)
    grouped = qkv_whole.reshape(3, qkv_whole.shape[1], groups, -1)
    partial_value = jnp.einsum("tsgc,sdgc->tgd", parts, grouped, preferred_element_type=jnp.float32)
    return jnp.sum(partial_value.astype(jnp.bfloat16), 1, dtype=jnp.float32)


def forward_layer(residual, matrices, gains, shifts, bias_pair, bias_hidden, branch_pair):
    w_qkv, w_out, w_up, w_down = matrices
    attn_in = normalize(residual, gains[0], shifts[0]).astype(jnp.bfloat16)

    def project_qkv(piece):
        return jnp.einsum("td,sdc->tsc", piece, w_qkv, preferred_element_type=jnp.float32)

    def project_up(piece):
        return jnp.dot(piece, w_up, preferred_element_type=jnp.float32)

    mixed_qkv = spread_only(attn_in, project_qkv)
    queries = (mixed_qkv[:, 0] + bias_pair[0]).astype(jnp.bfloat16)
    keys_now = mixed_qkv[:, 1].astype(jnp.bfloat16)
    values_now = (mixed_qkv[:, 2] + bias_pair[1]).astype(jnp.bfloat16)
    mixed, log_total = attend(queries, keys_now, values_now)
    attended = mixed.astype(jnp.bfloat16)
    qkv_whole, out_whole = (
        lax.all_gather(w_qkv, "tensor", axis=2, tiled=True),
        lax.all_gather(w_out, "tensor", axis=0, tiled=True),
    )
    token_att = lax.all_to_all(attended, "tensor", split_axis=0, concat_axis=1, tiled=True)
    attn_branch = group_rows(token_att, out_whole)
    middle = residual + attn_branch + branch_pair[0]
    mlp_in = normalize(middle, gains[1], shifts[1]).astype(jnp.bfloat16)
    raised = spread_only(mlp_in, project_up)
    hidden = raised + bias_hidden
    activated = gelu_exact(hidden).astype(jnp.bfloat16)
    result = middle + rows_sum(activated, w_down, "tc,cd->td") + branch_pair[1]
    saved = (
        residual,
        middle,
        attn_in,
        mlp_in,
        None,
        None,
        queries,
        keys_now,
        values_now,
        log_total,
        attended,
        hidden,
        activated,
        qkv_whole,
    )
    return (result, saved)


def backward_layer(grad_residual, saved, matrices, gains, shifts):
    w_qkv, w_out, w_up, w_down = matrices
    (
        residual,
        middle,
        attn_in,
        mlp_in,
        attn_rows,
        mlp_rows,
        queries,
        keys_now,
        values_now,
        log_total,
        attended,
        hidden,
        activated,
        qkv_whole,
    ) = saved
    down_bias_grad = jnp.sum(grad_residual, 0)

    def back_down(piece):
        return jnp.einsum("td,fd->tf", piece, w_down, preferred_element_type=jnp.float32)

    gathered_out, grad_act = spread_grads(grad_residual.astype(jnp.bfloat16), back_down)
    down_grad = jnp.einsum("tf,td->fd", activated, gathered_out, preferred_element_type=jnp.float32)
    grad_hidden = jax.vjp(gelu_exact, hidden)[1](grad_act)[0].astype(jnp.bfloat16)
    up_bias_grad = jnp.sum(grad_hidden, 0, dtype=jnp.float32)
    up_grad = fold_again(mlp_in, grad_hidden)
    grad_mlp_in = grads_sum(grad_hidden, w_up, "tf,df->td")
    norm_back = jax.vjp(normalize, middle, gains[1], shifts[1])[1]
    grad_norm, gain_second, shift_second = norm_back(grad_mlp_in)
    grad_middle = grad_residual + grad_norm
    attn_bias_grad = jnp.sum(grad_middle, 0)

    def back_out(piece):
        return jnp.einsum("td,cd->tc", piece, w_out, preferred_element_type=jnp.float32)

    gathered_mid, grad_attended = spread_grads(grad_middle.astype(jnp.bfloat16), back_out)
    out_grad = jnp.einsum("tc,td->cd", attended, gathered_mid, preferred_element_type=jnp.float32)
    grad_query, grad_key, grad_value = attend_back(
        queries, keys_now, values_now, log_total, grad_attended.astype(jnp.bfloat16)
    )
    grad_query = grad_query.astype(jnp.bfloat16)
    grad_key = grad_key.astype(jnp.bfloat16)
    grad_value = grad_value.astype(jnp.bfloat16)
    pair_grad = jnp.stack(
        [jnp.sum(grad_query, 0, dtype=jnp.float32), jnp.sum(grad_value, 0, dtype=jnp.float32)]
    )
    stacked = jnp.stack([grad_query, grad_key, grad_value], 1)
    flat_grad = fold_again(attn_in, stacked.reshape(stacked.shape[0], -1))
    qkv_grad = jnp.transpose(flat_grad.reshape(flat_grad.shape[0], 3, -1), (1, 0, 2))
    token_grads = lax.all_to_all(stacked, "tensor", split_axis=0, concat_axis=2, tiled=True)
    grad_attn_in = group_grads(token_grads, qkv_whole)
    first_back = jax.vjp(normalize, residual, gains[0], shifts[0])[1]
    grad_first, gain_first, shift_first = first_back(grad_attn_in)
    grad_input = grad_middle + grad_first
    matrix_part = (qkv_grad[None], out_grad[None], up_grad[None], down_grad[None])
    shared_part = (
        jnp.stack([gain_first, gain_second]),
        jnp.stack([shift_first, shift_second]),
        jnp.stack([attn_bias_grad, down_bias_grad]),
    )
    head_part = (pair_grad, up_bias_grad)
    return (grad_input, matrix_part, shared_part, head_part)


def body(
    inputs, w_qkv, w_out, w_up, w_down, ln_gain, ln_bias, bias_qv, bias_up, branch_bias, cotangent
):
    residual = inputs.astype(jnp.float32)
    saved_all = []
    for layer in range(LAYERS):
        matrices = layer_weights(w_qkv, w_out, w_up, w_down, layer)
        residual, saved = forward_layer(
            residual,
            matrices,
            ln_gain[layer],
            ln_bias[layer],
            bias_qv[layer],
            bias_up[layer],
            branch_bias[layer],
        )
        saved_all.append(saved)
    outputs = residual.astype(jnp.bfloat16)
    grad_residual = cotangent
    matrix_grads = [None] * LAYERS
    shared_grads = [None] * LAYERS
    head_grads = [None] * LAYERS
    for layer in reversed(range(LAYERS)):
        matrices = layer_weights(w_qkv, w_out, w_up, w_down, layer)
        grad_residual, matrix_part, shared_part, head_part = backward_layer(
            grad_residual, saved_all[layer], matrices, ln_gain[layer], ln_bias[layer]
        )
        matrix_grads[layer] = return_grads(
            matrix_part[0], matrix_part[1], matrix_part[2], matrix_part[3]
        )
        shared_grads[layer] = shared_part
        head_grads[layer] = head_part
    joined = [jnp.concatenate([grads[index] for grads in matrix_grads], 0) for index in range(4)]
    gain_total = jnp.stack([grads[0] for grads in shared_grads])
    shift_total = jnp.stack([grads[1] for grads in shared_grads])
    branch_total = jnp.stack([grads[2] for grads in shared_grads])
    gain_sum, shift_sum, branch_sum = lax.psum(
        (gain_total, shift_total, branch_total), ("dp", "tensor")
    )
    pair_total = jnp.stack([grads[0] for grads in head_grads])
    hidden_total = jnp.stack([grads[1] for grads in head_grads])
    pair_sum, hidden_sum = lax.psum((pair_total, hidden_total), "dp")
    return (
        outputs,
        grad_residual,
        joined[0],
        joined[1],
        joined[2],
        joined[3],
        gain_sum,
        shift_sum,
        pair_sum,
        hidden_sum,
        branch_sum,
    )


def solution(mesh):
    return jax.shard_map(
        body,
        mesh=mesh,
        in_specs=(
            P(("dp", "tensor"), None),
            P(None, None, "dp", "tensor"),
            P(None, "tensor", "dp"),
            P(None, "dp", "tensor"),
            P(None, "tensor", "dp"),
            P(),
            P(),
            P(None, None, "tensor"),
            P(None, "tensor"),
            P(),
            P(("dp", "tensor"), None),
        ),
        out_specs=(
            P(("dp", "tensor"), None),
            P(("dp", "tensor"), None),
            P(None, None, "dp", "tensor"),
            P(None, "tensor", "dp"),
            P(None, "dp", "tensor"),
            P(None, "tensor", "dp"),
            P(),
            P(),
            P(None, None, "tensor"),
            P(None, "tensor"),
            P(),
        ),
        check_vma=False,
    )
```

profile of v0, /device:TPU:12, one launch (start us, length us, event | category | flops | bytes accessed | tf_op | source)
XLA Modules:
  0.0 1674.3 jit_solution(17339127591960681586)
XLA Ops:
  16.2 14.7 all_gather.71
  31.0 55.3 %all-gather.15.cloned.1.call-done = bf16[6144,512]{1,0:T(8,128)(2,1)} async-done(((bf16[1536,512]{1,0:T(8,128)(2,1)}), bf16[6144,512]{1,0:T(8,128)(2,1)}) %all-gather.15.cloned.1.call-update) | async-done | bytes 6291472 | tf_op jit(solution)/shard_map/all_gather | solution.py:170
  86.3 5.5 fusion.18
  127.3 5.7 copy.448
  132.9 6.3 reshape.482
  144.1 14.0 all_gather.72
  158.7 10.3 all-gather
  178.9 15.7 all_gather.75
  194.6 16.1 all_gather.76
  210.7 36.6 %all-gather.17.cloned.1.call-done = bf16[6144,512]{1,0:T(8,128)(2,1)} async-done(((bf16[1536,512]{1,0:T(8,128)(2,1)}), bf16[6144,512]{1,0:T(8,128)(2,1)}) %all-gather.17.cloned.1.call-update) | async-done | bytes 6291472 | tf_op jit(solution)/shard_map/all_gather | solution.py:170
  247.2 33.3 %multiply_convert_fusion.1 = (bf16[6144,512]{1,0:T(8,128)(2,1)S(1)}, f32[6144,512]{1,0:T(8,128)}, f32[6144,512]{1,0:T(8,128)}) fusion(f32[512]{0:T(512)S(1)} %bitcast.514, bf16[6144,512]{1,0:T(8,128)(2,1)} %all-gather.17.cloned.1.call-done, bf16[1,512,512]{2,1,0:T(8,128)(2,1)} %all_gather.75), kind=kOutput, calls=%fused_computation.28 | convolution fusion | flops 3428843520 | bytes 38275072 | tf_op jit(solution)/shard_map/dot_general | solution.py:233
  283.3 5.4 convolution_convert_fusion.3
  288.7 70.2 %reduce-scatter.21.cloned.1.call-done = bf16[1536,512]{1,0:T(8,128)(2,1)} async-done(((bf16[6144,512]{1,0:T(8,128)(2,1)}), bf16[1536,512]{1,0:T(8,128)(2,1)}) %reduce-scatter.21.cloned.1.call-update) | async-done | bytes 1572880 | tf_op jit(solution)/shard_map/reduce_scatter | solution.py:192
  364.4 14.9 all_gather.78
  379.3 55.4 %all-gather.19.cloned.1.call-done = bf16[6144,512]{1,0:T(8,128)(2,1)} async-done(((bf16[1536,512]{1,0:T(8,128)(2,1)}), bf16[6144,512]{1,0:T(8,128)(2,1)}) %all-gather.19.cloned.1.call-update) | async-done | bytes 6291472 | tf_op jit(solution)/shard_map/all_gather | solution.py:170
  434.7 5.5 fusion.14
  475.7 5.7 copy.449
  481.4 6.3 reshape.483
  487.7 4.9 all-to-all-start.1
  492.5 14.0 all_gather.79
  507.2 10.9 all-gather.1
  530.8 15.2 all_gather.82
  545.9 15.1 all_gather.83
  561.1 37.8 %all-gather.21.cloned.1.call-done = bf16[6144,512]{1,0:T(8,128)(2,1)} async-done(((bf16[1536,512]{1,0:T(8,128)(2,1)}), bf16[6144,512]{1,0:T(8,128)(2,1)}) %all-gather.21.cloned.1.call-update) | async-done | bytes 6291472 | tf_op jit(solution)/shard_map/all_gather | solution.py:170
  598.8 33.1 %multiply_convert_fusion = (bf16[6144,512]{1,0:T(8,128)(2,1)}, f32[6144,512]{1,0:T(8,128)}, f32[6144,512]{1,0:T(8,128)}) fusion(f32[512]{0:T(512)S(1)} %bitcast.517, bf16[6144,512]{1,0:T(8,128)(2,1)} %all-gather.21.cloned.1.call-done, bf16[1,512,512]{2,1,0:T(8,128)(2,1)S(1)} %all_gather.82), kind=kOutput, calls=%fused_computation.14 | convolution fusion | flops 3428843520 | bytes 38275072 | tf_op jit(solution)/shard_map/dot_general | solution.py:233
  631.9 38.8 %all-gather.23.cloned.1.call-done = bf16[6144,512]{1,0:T(8,128)(2,1)} async-done(((bf16[1536,512]{1,0:T(8,128)(2,1)}), bf16[6144,512]{1,0:T(8,128)(2,1)}) %all-gather.23.cloned.1.call-update) | async-done | bytes 6291472 | tf_op jit(solution)/shard_map/all_gather | solution.py:183
  670.7 14.1 convert_reduce_fusion.4
  687.5 5.4 convolution_convert_fusion.1
  693.0 8.3 convolution_convert_fusion.2
  701.7 61.4 %reduce-scatter.25.cloned.1.call-done = bf16[1536,512]{1,0:T(8,128)(2,1)} async-done(((bf16[6144,512]{1,0:T(8,128)(2,1)}), bf16[1536,512]{1,0:T(8,128)(2,1)}) %reduce-scatter.25.cloned.1.call-update) | async-done | bytes 1572880 | tf_op jit(solution)/shard_map/reduce_scatter | solution.py:201
  768.9 67.4 %reduce-scatter.23.cloned.1.call-done = bf16[1536,512]{1,0:T(8,128)(2,1)} async-done(((bf16[6144,512]{1,0:T(8,128)(2,1)}), bf16[1536,512]{1,0:T(8,128)(2,1)}) %reduce-scatter.23.cloned.1.call-update) | async-done | bytes 1572880 | tf_op jit(solution)/shard_map/reduce_scatter | solution.py:192
  836.3 5.1 fusion.269
  844.5 70.4 %all-gather.25.cloned.1.call-done = bf16[6144,512]{1,0:T(8,128)(2,1)} async-done(((bf16[1536,512]{1,0:T(8,128)(2,1)}), bf16[6144,512]{1,0:T(8,128)(2,1)}) %all-gather.25.cloned.1.call-update) | async-done | bytes 6291472 | tf_op jit(solution)/shard_map/all_gather | solution.py:183
  915.0 5.8 convolution_convert_fusion.5
  928.7 4.6 multiply_reduce_fusion.1
  945.5 6.5 multiply_convert_fusion.3
  962.9 5.2 convert_reduce_fusion.12
  976.1 10.1 copy.393
  986.2 5.8 all-to-all-start.2
  992.6 68.5 %all-gather.31.cloned.1.call-done = bf16[1,3,512,512]{3,2,1,0:T(8,128)(2,1)} async-done(((bf16[1,3,512,128]{3,2,1,0:T(8,128)(2,1)}), bf16[1,3,512,512]{3,2,1,0:T(8,128)(2,1)}) %all-gather.31.cloned.1.call-update) | async-done | bytes 1572880 | tf_op jit(solution)/shard_map/all_gather | solution.py:242
  1063.7 10.6 all-to-all-done.2
  1077.8 5.1 convert_reduce_fusion.2
  1090.3 72.9 %all-gather.27.cloned.1.call-done = bf16[6144,512]{1,0:T(8,128)(2,1)} async-done(((bf16[1536,512]{1,0:T(8,128)(2,1)}), bf16[6144,512]{1,0:T(8,128)(2,1)}) %all-gather.27.cloned.1.call-update) | async-done | bytes 6291472 | tf_op jit(solution)/shard_map/all_gather | solution.py:183
  1163.2 13.4 convert_reduce_fusion.5
  1179.3 5.3 convolution_convert_fusion
  1185.8 8.8 fusion.149
  1200.9 54.0 %reduce-scatter.27.cloned.1.call-done = bf16[1536,512]{1,0:T(8,128)(2,1)} async-done(((bf16[6144,512]{1,0:T(8,128)(2,1)}), bf16[1536,512]{1,0:T(8,128)(2,1)}) %reduce-scatter.27.cloned.1.call-update) | async-done | bytes 1572880 | tf_op jit(solution)/shard_map/reduce_scatter | solution.py:201
  1271.3 8.0 fusion.148
  1281.5 6.2 all-gather.33.cloned.1.call-done
  1293.9 8.9 fusion.147
  1302.8 14.4 reduce-scatter.43.cloned.1.call-done
  1318.3 8.9 fusion.146
  1327.2 63.8 %all-gather.29.cloned.1.call-done = bf16[6144,512]{1,0:T(8,128)(2,1)} async-done(((bf16[1536,512]{1,0:T(8,128)(2,1)}), bf16[6144,512]{1,0:T(8,128)(2,1)}) %all-gather.29.cloned.1.call-update) | async-done | bytes 6291472 | tf_op jit(solution)/shard_map/all_gather | solution.py:183
  1391.1 5.7 convolution_convert_fusion.4
  1444.5 10.2 copy.417
  1454.7 5.9 all-to-all-start.3
  1465.4 7.7 fusion.150
  1476.4 7.7 fusion.155
  1484.2 30.2 %reduce-scatter.33.cloned.1.call-done = bf16[1,64,512]{2,1,0:T(8,128)(2,1)} async-done(((bf16[1,512,512]{2,1,0:T(8,128)(2,1)}), bf16[1,64,512]{2,1,0:T(8,128)(2,1)}) %reduce-scatter.33.cloned.1.call-update) | async-done | bytes 65552 | tf_op jit(solution)/shard_map/reduce_scatter | solution.py:150
  1516.2 14.9 all-reduce.1
  1531.1 13.9 reduce-scatter.37.cloned.1.call-done
  1546.6 29.4 %reduce-scatter.31.cloned.1.call-done = bf16[1,3,64,128]{3,2,1,0:T(8,128)(2,1)} async-done(((bf16[1,3,512,128]{3,2,1,0:T(8,128)(2,1)}), bf16[1,3,64,128]{3,2,1,0:T(8,128)(2,1)}) %reduce-scatter.31.cloned.1.call-update) | async-done | bytes 49168 | tf_op jit(solution)/shard_map/reduce_scatter | solution.py:144
  1576.0 31.2 %reduce-scatter.29.cloned.1.call-done = bf16[1,3,64,128]{3,2,1,0:T(8,128)(2,1)} async-done(((bf16[1,3,512,128]{3,2,1,0:T(8,128)(2,1)}), bf16[1,3,64,128]{3,2,1,0:T(8,128)(2,1)}) %reduce-scatter.29.cloned.1.call-update) | async-done | bytes 49168 | tf_op jit(solution)/shard_map/reduce_scatter | solution.py:144
  1622.8 44.5 %all-reduce = (f32[2,2,512]{2,1,0:T(2,128)}, f32[2,2,512]{2,1,0:T(2,128)}, f32[2,2,512]{2,1,0:T(2,128)}) all-reduce(f32[2,2,512]{2,1,0:T(2,128)S(1)} %pad_maximum_fusion, f32[2,2,512]{2,1,0:T(2,128)S(1)} %pad_maximum_fusion.1, f32[2,2,512]{2,1,0:T(2,128)S(1)} %pad_maximum_fusion.2), channel_id=1, replica_groups=mesh['dp'=8,'tensor'=4] {'dp','tensor'}, use_global_device_ids=true, to_apply=%region_52.53 | all-reduce | flops 6144 | bytes 49152 | tf_op jit(solution)/shard_map/psum | solution.py:374
  (520 shorter events, 291.1 us)
Async XLA Ops:
  7.2 79.1 %all-gather.15.cloned.1.call-start = ((), (), s32[]{:S(2)}) async-start(), calls=%async_computation.16 | async-start | bytes 7864320 | tf_op jit(solution)/shard_map/all_gather | solution.py:170
  12.4 162.7 %copy-start.95 = (f32[1,1,512]{2,1,0:T(1,128)}, f32[1,1,512]{2,1,0:T(1,128)S(1)}, u32[]{:S(2)}) copy-start(f32[1,1,512]{2,1,0:T(1,128)S(1)} %get-tuple-element.137) | copy-start | bytes 6148
  15.6 92.5 %copy-start.115 = (pred[16,16]{1,0:T(8,128)(4,1)}, pred[16,16]{1,0:T(8,128)(4,1)S(1)}, u32[]{:S(2)}) copy-start(pred[16,16]{1,0:T(8,128)(4,1)S(1)} %iota_compare_fusion.1) | copy-start | bytes 772
  31.0 60.8 %copy-start.48 = (bf16[1,3,512,128]{3,2,1,0:T(8,128)(2,1)}, bf16[1,3,512,128]{3,2,1,0:T(8,128)(2,1)S(1)}, u32[]{:S(2)}) copy-start(bf16[1,3,512,128]{3,2,1,0:T(8,128)(2,1)S(1)} %all_gather.71) | copy-start | bytes 1179652
  109.0 15.5 copy-start.17
  127.2 12.0 copy-start.27
  132.9 10.5 copy-start.98
  139.2 30.0 %copy-start.112 = (f32[2,2,512]{2,1,0:T(2,128)S(1)}, f32[2,2,512]{2,1,0:T(2,128)}, u32[]{:S(2)}) copy-start(f32[2,2,512]{2,1,0:T(2,128)} %param.20) | copy-start | bytes 24580
  139.2 30.6 %all-to-all-start = ((bf16[4,1536,128]{2,1,0:T(8,128)(2,1)}), bf16[4,1536,128]{2,1,0:T(8,128)(2,1)S(1)}, u32[]{:S(2)}, u32[]{:S(2)}) async-start(bf16[4,1536,128]{2,1,0:T(8,128)(2,1)} %reshape.482), calls=%async_computation | async-start | bytes 3145728 | tf_op jit(solution)/shard_map/all_to_all | solution.py:245
  143.5 103.8 %all-gather.17.cloned.1.call-start = ((), (), s32[]{:S(2)}) async-start(), calls=%async_computation.17 | async-start | bytes 7864320 | tf_op jit(solution)/shard_map/all_gather | solution.py:170
  173.6 185.3 %copy-start = (f32[1536,512]{1,0:T(8,128)}, f32[1536,512]{1,0:T(8,128)S(1)}, u32[]{:S(2)}) copy-start(f32[1536,512]{1,0:T(8,128)S(1)} %get-tuple-element.114) | copy-start | bytes 9437188
  176.9 182.0 %reduce-scatter.21.cloned.1.call-start = ((), (), s32[]{:S(2)}) async-start(), calls=%async_computation.18 | async-start | bytes 7864320 | tf_op jit(solution)/shard_map/reduce_scatter | solution.py:192
  177.6 103.0 %copy-start.118 = (f32[1,512]{1,0:T(1,128)}, f32[1,512]{1,0:T(1,128)S(1)}, u32[]{:S(2)}) copy-start(f32[1,512]{1,0:T(1,128)S(1)} %get-tuple-element.145) | copy-start | bytes 6148
  247.2 36.1 %copy-start.58 = (bf16[1,512,512]{1,2,0:T(8,128)(2,1)S(1)}, bf16[1,512,512]{1,2,0:T(8,128)(2,1)}, u32[]{:S(2)}) copy-start(bf16[1,512,512]{1,2,0:T(8,128)(2,1)} %all_gather.76) | copy-start | bytes 1572868
  288.7 146.0 %all-gather.19.cloned.1.call-start = ((), (), s32[]{:S(2)}) async-start(), calls=%async_computation.19 | async-start | bytes 7864320 | tf_op jit(solution)/shard_map/all_gather | solution.py:170
  379.3 60.9 %copy-start.49 = (bf16[1,3,512,128]{3,2,1,0:T(8,128)(2,1)}, bf16[1,3,512,128]{3,2,1,0:T(8,128)(2,1)S(1)}, u32[]{:S(2)}) copy-start(bf16[1,3,512,128]{3,2,1,0:T(8,128)(2,1)S(1)} %all_gather.78) | copy-start | bytes 1179652
  457.3 15.6 copy-start.19
  475.7 12.0 copy-start.29
  481.4 11.1 copy-start.92
  487.7 32.7 %all-to-all-start.1 = ((bf16[4,1536,128]{2,1,0:T(8,128)(2,1)}), bf16[4,1536,128]{2,1,0:T(8,128)(2,1)}, u32[]{:S(2)}, u32[]{:S(2)}) async-start(bf16[4,1536,128]{2,1,0:T(8,128)(2,1)} %reshape.483), calls=%async_computation.2 | async-start | bytes 3145728 | tf_op jit(solution)/shard_map/all_to_all | solution.py:245
  492.5 106.3 %all-gather.21.cloned.1.call-start = ((), (), s32[]{:S(2)}) async-start(), calls=%async_computation.20 | async-start | bytes 7864320 | tf_op jit(solution)/shard_map/all_gather | solution.py:170
  527.9 18.0 %copy-start.69 = (bf16[1,512,64]{1,2,0:T(8,128)(2,1)S(1)}, bf16[1,512,64]{1,2,0:T(8,128)(2,1)}, u32[]{:S(2)}) copy-start(bf16[1,512,64]{1,2,0:T(8,128)(2,1)} %get-tuple-element.124) | copy-start | bytes 196612
  527.9 70.9 %copy-start.120 = (f32[1,512]{1,0:T(1,128)S(1)}, f32[1,512]{1,0:T(1,128)}, u32[]{:S(2)}) copy-start(f32[1,512]{1,0:T(1,128)} %get-tuple-element.144) | copy-start | bytes 6148
  527.9 142.8 %all-gather.23.cloned.1.call-start = ((), (), s32[]{:S(2)}) async-start(), calls=%async_computation.22 | async-start | bytes 7864320 | tf_op jit(solution)/shard_map/all_gather | solution.py:183
  530.7 232.4 %reduce-scatter.25.cloned.1.call-start = ((), (), s32[]{:S(2)}) async-start(), calls=%async_computation.23 | async-start | bytes 7864320 | tf_op jit(solution)/shard_map/reduce_scatter | solution.py:201
  692.9 143.4 %reduce-scatter.23.cloned.1.call-start = ((), (), s32[]{:S(2)}) async-start(), calls=%async_computation.21 | async-start | bytes 7864320 | tf_op jit(solution)/shard_map/reduce_scatter | solution.py:192
  701.2 61.9 %copy-start.6 = (f32[1536,512]{1,0:T(8,128)S(1)}, f32[1536,512]{1,0:T(8,128)}, u32[]{:S(2)}) copy-start(f32[1536,512]{1,0:T(8,128)} %copy-done.5) | copy-start | bytes 9437188
  701.3 213.7 %all-gather.25.cloned.1.call-start = ((), (), s32[]{:S(2)}) async-start(), calls=%async_computation.24 | async-start | bytes 7864320 | tf_op jit(solution)/shard_map/all_gather | solution.py:183
  766.4 69.9 %copy-start.107 = (f32[1,1,512]{2,1,0:T(1,128)S(1)}, f32[1,1,512]{2,1,0:T(1,128)}, u32[]{:S(2)}) copy-start(f32[1,1,512]{2,1,0:T(1,128)} %get-tuple-element.132) | copy-start | bytes 6148
  843.1 71.9 %copy-start.56 = (bf16[1,128,512]{1,2,0:T(8,128)(2,1)S(1)}, bf16[1,128,512]{1,2,0:T(8,128)(2,1)}, u32[]{:S(2)}) copy-start(bf16[1,128,512]{1,2,0:T(8,128)(2,1)} %copy-done.55) | copy-start | bytes 393220
  920.8 7.9 slice-start.2
  945.5 6.5 copy-start.24
  986.2 88.0 %all-to-all-start.2 = ((bf16[6144,3,128]{2,1,0:T(4,128)(2,1)}), bf16[6144,3,128]{2,1,0:T(4,128)(2,1)}, u32[]{:S(2)}, u32[]{:S(2)}) async-start(bf16[6144,3,128]{2,1,0:T(4,128)(2,1)} %copy.393), calls=%async_computation.5 | async-start | bytes 12582912 | tf_op jit(solution)/shard_map/all_to_all | solution.py:323
  992.0 69.1 %all-gather.31.cloned.1.call-start = ((), (), s32[]{:S(2)}) async-start(), calls=%async_computation.32 | async-start | bytes 1966080 | tf_op jit(solution)/shard_map/all_gather | solution.py:242
  992.6 170.6 %all-gather.27.cloned.1.call-start = ((), (), s32[]{:S(2)}) async-start(), calls=%async_computation.25 | async-start | bytes 7864320 | tf_op jit(solution)/shard_map/all_gather | solution.py:183
  1088.9 74.3 %copy-start.59 = (bf16[1,512,512]{1,2,0:T(8,128)(2,1)S(1)}, bf16[1,512,512]{1,2,0:T(8,128)(2,1)}, u32[]{:S(2)}) copy-start(bf16[1,512,512]{1,2,0:T(8,128)(2,1)} %all_gather.76) | copy-start | bytes 1572868
  1088.9 74.3 %copy-start.119 = (f32[1,512]{1,0:T(1,128)S(1)}, f32[1,512]{1,0:T(1,128)}, u32[]{:S(2)}) copy-start(f32[1,512]{1,0:T(1,128)} %copy-done.118) | copy-start | bytes 6148
  1090.2 164.6 %reduce-scatter.27.cloned.1.call-start = ((), (), s32[]{:S(2)}) async-start(), calls=%async_computation.26 | async-start | bytes 7864320 | tf_op jit(solution)/shard_map/reduce_scatter | solution.py:201
  1163.2 16.1 copy-start.57
  1184.6 103.1 %all-gather.33.cloned.1.call-start = ((), (), s32[]{:S(2)}) async-start(), calls=%async_computation.33 | async-start | bytes 1966080 | tf_op jit(solution)/shard_map/all_gather | solution.py:242
  1185.4 131.8 %reduce-scatter.43.cloned.1.call-start = ((), (), s32[]{:S(2)}) async-start(), calls=%async_computation.37 | async-start | bytes 589824
  1194.7 60.2 %copy-start.1 = (f32[1536,512]{1,0:T(8,128)S(1)}, f32[1536,512]{1,0:T(8,128)}, u32[]{:S(2)}) copy-start(f32[1536,512]{1,0:T(8,128)} %copy-done) | copy-start | bytes 9437188
  1194.7 60.2 %copy-start.67 = (f32[1536]{0:T(1024)S(1)}, f32[1536]{0:T(1024)}, u32[]{:S(2)}) copy-start(f32[1536]{0:T(1024)} %copy-done.66) | copy-start | bytes 18436
  1194.7 60.2 %copy-start.96 = (f32[1,1,512]{2,1,0:T(1,128)S(1)}, f32[1,1,512]{2,1,0:T(1,128)}, u32[]{:S(2)}) copy-start(f32[1,1,512]{2,1,0:T(1,128)} %copy-done.95) | copy-start | bytes 6148
  1198.4 59.1 %copy-start.89 = (f32[1536]{0:T(1024)S(1)}, f32[1536]{0:T(1024)}, u32[]{:S(2)}) copy-start(f32[1536]{0:T(1024)} %copy-done.88) | copy-start | bytes 18436
  1198.4 59.2 %copy-start.80 = (f32[1536]{0:T(1024)S(1)}, f32[1536]{0:T(1024)}, u32[]{:S(2)}) copy-start(f32[1536]{0:T(1024)} %copy-done.79) | copy-start | bytes 18436
  1200.8 190.2 %all-gather.29.cloned.1.call-start = ((), (), s32[]{:S(2)}) async-start(), calls=%async_computation.27 | async-start | bytes 7864320 | tf_op jit(solution)/shard_map/all_gather | solution.py:183
  1264.2 209.2 %reduce-scatter.39.cloned.1.call-start = ((), (), s32[]{:S(2)}) async-start(), calls=%async_computation.35 | async-start | bytes 147456
  1271.3 203.1 %reduce-scatter.41.cloned.1.call-start = ((), (), s32[]{:S(2)}) async-start(), calls=%async_computation.36 | async-start | bytes 589824
  1279.4 11.9 copy-start.28
  1281.3 11.0 copy-start.51
  1281.3 202.9 %reduce-scatter.35.cloned.1.call-start = ((), (), s32[]{:S(2)}) async-start(), calls=%async_computation.31 | async-start | bytes 589824 | tf_op jit(solution)/shard_map/reduce_scatter | solution.py:150
  1302.8 211.6 %reduce-scatter.33.cloned.1.call-start = ((), (), s32[]{:S(2)}) async-start(), calls=%async_computation.30 | async-start | bytes 589824 | tf_op jit(solution)/shard_map/reduce_scatter | solution.py:150
  1318.3 72.8 %copy-start.54 = (bf16[1,128,512]{1,2,0:T(8,128)(2,1)S(1)}, bf16[1,128,512]{1,2,0:T(8,128)(2,1)}, u32[]{:S(2)}) copy-start(bf16[1,128,512]{1,2,0:T(8,128)(2,1)} %copy-done.53) | copy-start | bytes 393220
  1396.8 8.1 slice-start
  1454.7 154.0 %all-to-all-start.3 = ((bf16[6144,3,128]{2,1,0:T(4,128)(2,1)}), bf16[6144,3,128]{2,1,0:T(4,128)(2,1)}, u32[]{:S(2)}, u32[]{:S(2)}) async-start(bf16[6144,3,128]{2,1,0:T(4,128)(2,1)} %copy.417), calls=%async_computation.7 | async-start | bytes 12582912 | tf_op jit(solution)/shard_map/all_to_all | solution.py:323
  1460.6 84.4 %reduce-scatter.37.cloned.1.call-start = ((), (), s32[]{:S(2)}) async-start(), calls=%async_computation.34 | async-start | bytes 147456
  1465.3 7.8 copy-start.122
  1465.3 7.9 copy-start.123
  1465.3 8.9 copy-start.117
  1465.3 110.7 %reduce-scatter.31.cloned.1.call-start = ((), (), s32[]{:S(2)}) async-start(), calls=%async_computation.29 | async-start | bytes 442368 | tf_op jit(solution)/shard_map/reduce_scatter | solution.py:144
  1473.3 133.8 %reduce-scatter.29.cloned.1.call-start = ((), (), s32[]{:S(2)}) async-start(), calls=%async_computation.28 | async-start | bytes 442368 | tf_op jit(solution)/shard_map/reduce_scatter | solution.py:144
  1476.4 39.6 %copy-start.103 = (f32[512]{0:T(512)S(1)}, f32[512]{0:T(512)}, u32[]{:S(2)}) copy-start(f32[512]{0:T(512)} %get-tuple-element.121) | copy-start | bytes 6148
  1476.4 39.6 %copy-start.104 = (f32[512]{0:T(512)S(1)}, f32[512]{0:T(512)}, u32[]{:S(2)}) copy-start(f32[512]{0:T(512)} %get-tuple-element.95) | copy-start | bytes 6148
  (95 other events, 291.1 us)
Sparse Core Ops, SparseCore 0:
  15.0 71.2 all-gather.14
  177.1 70.1 all-gather.16
  288.8 70.0 reduce-scatter.20
  364.3 70.3 all-gather.18
  528.0 70.7 all-gather.20
  600.5 70.1 all-gather.22
  693.0 70.0 reduce-scatter.24
  766.1 70.1 reduce-scatter.22
  844.6 70.3 all-gather.24
  994.3 66.7 all-gather.30
  1090.4 72.8 all-gather.26
  1184.8 70.0 reduce-scatter.26
  1256.7 30.9 all-gather.32
  1289.8 27.3 reduce-scatter.42
  1319.1 71.9 all-gather.28
  1393.8 26.6 reduce-scatter.38
  1422.6 28.9 reduce-scatter.40
  1453.8 29.1 reduce-scatter.34
  1485.3 29.0 reduce-scatter.32
  1516.5 28.3 reduce-scatter.36
  1547.2 28.7 reduce-scatter.30
  1578.4 28.7 reduce-scatter.28
where the time goes:
time: 1690 us; the launch traced here: 1670 us
  waiting for transfers between devices  890 us (53%)
  matrix products  278 us (16%)
  blocking collectives  200 us (12%)
  local copies, waits for them, and re-layouts  189 us (11%)
  other arithmetic  78.1 us (5%)
  starting transfers between devices  22.5 us (1%)
    all_gather x4, waiting for transfers between devices, spread_grads(): piece = lax.all_gather(rows, 'tensor', axis=0, tiled=True)  246 us
    all_gather x4, waiting for transfers between devices, spread_only(): return project(lax.all_gather(rows, 'tensor', axis=0, tiled=True))  185 us
    reduce_scatter x2, waiting for transfers between devices, rows_sum(): lax.psum_scatter(slice_term(source, weight, form).astype(jnp.bfloat16), '...  138 us
    reduce_scatter x2, waiting for transfers between devices, grads_sum(): lax.psum_scatter(slice_term(source, weight, form).astype(jnp.bfloat16), '...  115 us
    all_gather x2, waiting for transfers between devices, forward_layer(): lax.all_gather(w_qkv, 'tensor', axis=2, tiled=True)  74.7 us
    dot_general x2, matrix products, project_up(): return jnp.dot(piece, w_up, preferred_element_type=jnp.float32)  66.4 us
    reduce_scatter x2, waiting for transfers between devices, return_grads(): lax.psum_scatter(first.astype(jnp.bfloat16), 'dp', scatter_dimension=2, t...  60.6 us
    unnamed x296, local copies, waits for them, and re-layouts  59.3 us
  transfers between devices with their start and end apart: 26, of which 20 were waited for; matrix products, arithmetic and copies ran while one was open for 13% of the time, Pallas kernels for 0%

commit v1 on v0

--- a/solution.py
+++ b/solution.py
@@ -180,7 +180,14 @@
 
 
 def spread_grads(rows, project):
-    piece = lax.all_gather(rows, "tensor", axis=0, tiled=True)
+    wide_out, t_next = (lax.axis_size("tensor"), lax.axis_index("tensor"))
+    piece, block_next = (rows, 1)
+    while block_next < wide_out:
+        spare = lax.ppermute(piece, "tensor", [(at, at ^ block_next) for at in range(wide_out)])
+        small = jnp.concatenate([piece, spare], axis=0)
+        w2 = jnp.concatenate([spare, piece], axis=0)
+        piece = jnp.where(t_next & block_next == 0, small, w2)
+        block_next = 2 * block_next
     return (piece, project(piece))
 
 

time: 1690 us -> 1730 us (1.024)
  waiting for transfers between devices: 890 us -> 920 us
  other arithmetic: 78.1 us -> 96.1 us
    ppermute x0 -> x8, waiting for transfers between devices: none -> 364 us  [spread_grads(): lax.ppermute(piece, 'tensor', [(at, at ^ block_next) for at in range(wide...]
    all_gather x4 -> x0, waiting for transfers between devices: 246 us -> none  [spread_grads(): piece = lax.all_gather(rows, 'tensor', axis=0, tiled=True)]
    dot_general x2, matrix products: 27.5 us -> 63 us  [back_down(): jnp.einsum('td,fd->tf', piece, w_down, preferred_element_type=jnp.float32)]
    reduce_scatter x2, waiting for transfers between devices: 30.2 us -> 0.04 us  [return_grads(): lax.psum_scatter(third.astype(jnp.bfloat16), 'dp', scatter_dimension=1, t...]
    unnamed x26 -> x22, waiting for transfers between devices: 29.9 us -> 1.58 us
    dot_general x2, matrix products: 66.4 us -> 39.1 us  [project_up(): return jnp.dot(piece, w_up, preferred_element_type=jnp.float32)]
    all_gather x4, waiting for transfers between devices: 185 us -> 162 us  [spread_only(): return project(lax.all_gather(rows, 'tensor', axis=0, tiled=True))]
    unnamed x296 -> x320, local copies, waits for them, and re-layouts: 59.3 us -> 50.2 us
  transfers between devices with their start and end apart: 26 -> 30, of which waited for: 20 -> 20; matrix products, arithmetic and copies ran while one was open for 13% -> 12% of each run, Pallas kernels for 0% -> 0%
where the time goes in v1:
time: 1730 us; the launch traced here: 1720 us
  waiting for transfers between devices  920 us (53%)
  matrix products  284 us (16%)
  blocking collectives  200 us (12%)
  local copies, waits for them, and re-layouts  175 us (10%)
  other arithmetic  96.1 us (6%)
  starting transfers between devices  31.3 us (2%)
    ppermute x8, waiting for transfers between devices, spread_grads(): lax.ppermute(piece, 'tensor', [(at, at ^ block_next) for at in range(wide...  364 us
    all_gather x4, waiting for transfers between devices, spread_only(): return project(lax.all_gather(rows, 'tensor', axis=0, tiled=True))  162 us
    reduce_scatter x2, waiting for transfers between devices, rows_sum(): lax.psum_scatter(slice_term(source, weight, form).astype(jnp.bfloat16), '...  138 us
    reduce_scatter x2, waiting for transfers between devices, grads_sum(): lax.psum_scatter(slice_term(source, weight, form).astype(jnp.bfloat16), '...  123 us
    all_gather x2, waiting for transfers between devices, forward_layer(): lax.all_gather(w_qkv, 'tensor', axis=2, tiled=True)  66.6 us
    dot_general x2, matrix products, back_down(): jnp.einsum('td,fd->tf', piece, w_down, preferred_element_type=jnp.float32)  63 us
    reduce_scatter x2, waiting for transfers between devices, return_grads(): lax.psum_scatter(first.astype(jnp.bfloat16), 'dp', scatter_dimension=2, t...  54.7 us
    unnamed x320, local copies, waits for them, and re-layouts  50.2 us
  transfers between devices with their start and end apart: 30, of which 20 were waited for; matrix products, arithmetic and copies ran while one was open for 12% of the time, Pallas kernels for 0%

profile of v1, /device:TPU:12, one launch (start us, length us, event | category | flops | bytes accessed | tf_op | source)
XLA Modules:
  0.0 1723.4 jit_solution(11724684884710507020)
XLA Ops:
  16.3 14.7 all_gather.59
  31.0 55.3 %all-gather.11.cloned.1.call-done = bf16[6144,512]{1,0:T(8,128)(2,1)} async-done(((bf16[1536,512]{1,0:T(8,128)(2,1)}), bf16[6144,512]{1,0:T(8,128)(2,1)}) %all-gather.11.cloned.1.call-update) | async-done | bytes 6291472 | tf_op jit(solution)/shard_map/all_gather | solution.py:170
  86.3 5.5 fusion.18
  119.6 5.7 copy.448
  125.2 6.3 reshape.482
  136.4 14.0 all_gather.60
  151.0 10.7 all-gather
  171.6 15.7 all_gather.64
  187.3 15.9 all_gather.63
  203.2 36.8 %all-gather.13.cloned.1.call-done = bf16[6144,512]{1,0:T(8,128)(2,1)} async-done(((bf16[1536,512]{1,0:T(8,128)(2,1)}), bf16[6144,512]{1,0:T(8,128)(2,1)}) %all-gather.13.cloned.1.call-update) | async-done | bytes 6291472 | tf_op jit(solution)/shard_map/all_gather | solution.py:170
  239.9 33.3 %multiply_convert_fusion.1 = (bf16[6144,512]{1,0:T(8,128)(2,1)S(1)}, f32[6144,512]{1,0:T(8,128)}, f32[6144,512]{1,0:T(8,128)}) fusion(f32[512]{0:T(512)S(1)} %bitcast.502, bf16[6144,512]{1,0:T(8,128)(2,1)} %all-gather.13.cloned.1.call-done, bf16[1,512,512]{2,1,0:T(8,128)(2,1)} %all_gather.63), kind=kOutput, calls=%fused_computation.28 | convolution fusion | flops 3428843520 | bytes 38275072 | tf_op jit(solution)/shard_map/dot_general | solution.py:240
  276.0 5.4 convolution_convert_fusion.3
  281.5 70.2 %reduce-scatter.21.cloned.1.call-done = bf16[1536,512]{1,0:T(8,128)(2,1)} async-done(((bf16[6144,512]{1,0:T(8,128)(2,1)}), bf16[1536,512]{1,0:T(8,128)(2,1)}) %reduce-scatter.21.cloned.1.call-update) | async-done | bytes 1572880 | tf_op jit(solution)/shard_map/reduce_scatter | solution.py:199
  357.1 14.7 all_gather.66
  371.9 55.6 %all-gather.15.cloned.1.call-done = bf16[6144,512]{1,0:T(8,128)(2,1)} async-done(((bf16[1536,512]{1,0:T(8,128)(2,1)}), bf16[6144,512]{1,0:T(8,128)(2,1)}) %all-gather.15.cloned.1.call-update) | async-done | bytes 6291472 | tf_op jit(solution)/shard_map/all_gather | solution.py:170
  427.4 5.5 fusion.14
  460.6 5.7 copy.449
  466.4 6.3 reshape.483
  477.6 14.0 all_gather.67
  492.2 11.3 all-gather.1
  517.4 54.7 %collective-permute-done = bf16[1536,512]{1,0:T(8,128)(2,1)} collective-permute-done((bf16[1536,512]{1,0:T(8,128)(2,1)}, bf16[1536,512]{1,0:T(8,128)(2,1)}, u32[]{:S(2)}, u32[]{:S(2)}) %collective-permute-start) | collective-permute-done | bytes 1572896 | tf_op jit(solution)/shard_map/ppermute | solution.py:186
  577.9 15.7 all_gather.71
  593.6 15.9 all_gather.70
  609.5 14.5 all-gather.17.cloned.1.call-done
  624.0 5.8 fusion.211
  629.8 37.2 %collective-permute-done.1 = bf16[3072,512]{1,0:T(8,128)(2,1)} collective-permute-done((bf16[3072,512]{1,0:T(8,128)(2,1)S(1)}, bf16[3072,512]{1,0:T(8,128)(2,1)}, u32[]{:S(2)}, u32[]{:S(2)}) %collective-permute-start.1) | collective-permute-done | bytes 3145760 | tf_op jit(solution)/shard_map/ppermute | solution.py:186
  667.0 41.9 %convert_reduce_fusion.4 = (f32[512]{0:T(512)}, bf16[6144,512]{1,0:T(8,128)(2,1)S(1)}, f32[6144,512]{1,0:T(8,128)}) fusion(f32[6144,512]{1,0:T(8,128)S(1)} %fusion.211, f32[512]{0:T(512)S(1)} %bitcast.481, bf16[1,512,512]{1,2,0:T(8,128)(2,1)S(1)} %copy-done.67, bf16[3072,512]{1,0:T(8,128)(2,1)} %collective-permute-done.1, ...), kind=kOutput, calls=%fused_computation.10 | convolution fusion | flops 3485466112 | bytes 38277120 | tf_op jit(solution)/shard_map/td,fd->tf/dot_general | solution.py:300
  711.5 5.3 convolution_convert_fusion.1
  717.1 10.2 multiply_convert_fusion
  730.0 5.4 convolution_convert_fusion.2
  735.5 52.6 %reduce-scatter.25.cloned.1.call-done = bf16[1536,512]{1,0:T(8,128)(2,1)} async-done(((bf16[6144,512]{1,0:T(8,128)(2,1)}), bf16[1536,512]{1,0:T(8,128)(2,1)}) %reduce-scatter.25.cloned.1.call-update) | async-done | bytes 1572880 | tf_op jit(solution)/shard_map/reduce_scatter | solution.py:208
  793.8 67.4 %reduce-scatter.23.cloned.1.call-done = bf16[1536,512]{1,0:T(8,128)(2,1)} async-done(((bf16[6144,512]{1,0:T(8,128)(2,1)}), bf16[1536,512]{1,0:T(8,128)(2,1)}) %reduce-scatter.23.cloned.1.call-update) | async-done | bytes 1572880 | tf_op jit(solution)/shard_map/reduce_scatter | solution.py:199
  867.3 35.4 %collective-permute-done.2 = bf16[1536,512]{1,0:T(8,128)(2,1)S(1)} collective-permute-done((bf16[1536,512]{1,0:T(8,128)(2,1)S(1)}, bf16[1536,512]{1,0:T(8,128)(2,1)S(1)}, u32[]{:S(2)}, u32[]{:S(2)}) %collective-permute-start.2) | collective-permute-done | bytes 1572896 | tf_op jit(solution)/shard_map/ppermute | solution.py:186
  904.5 68.2 %collective-permute-done.3 = bf16[3072,512]{1,0:T(8,128)(2,1)S(1)} collective-permute-done((bf16[3072,512]{1,0:T(8,128)(2,1)S(1)}, bf16[3072,512]{1,0:T(8,128)(2,1)S(1)}, u32[]{:S(2)}, u32[]{:S(2)}) %collective-permute-start.3) | collective-permute-done | bytes 3145760 | tf_op jit(solution)/shard_map/ppermute | solution.py:186
  974.4 6.9 convolution_convert_fusion.5
  1006.4 6.7 multiply_convert_fusion.3
  1033.1 10.1 copy.393
  1043.3 5.9 all-to-all-start.2
  1049.9 66.6 %all-gather.19.cloned.1.call-done = bf16[1,3,512,512]{3,2,1,0:T(8,128)(2,1)} async-done(((bf16[1,3,512,128]{3,2,1,0:T(8,128)(2,1)}), bf16[1,3,512,512]{3,2,1,0:T(8,128)(2,1)}) %all-gather.19.cloned.1.call-update) | async-done | bytes 1572880 | tf_op jit(solution)/shard_map/all_gather | solution.py:249
  1118.9 10.7 all-to-all-done.2
  1133.2 5.1 convert_reduce_fusion.2
  1146.5 34.6 %collective-permute-done.4 = bf16[1536,512]{1,0:T(8,128)(2,1)S(1)} collective-permute-done((bf16[1536,512]{1,0:T(8,128)(2,1)S(1)}, bf16[1536,512]{1,0:T(8,128)(2,1)S(1)}, u32[]{:S(2)}, u32[]{:S(2)}) %collective-permute-start.4) | collective-permute-done | bytes 1572896 | tf_op jit(solution)/shard_map/ppermute | solution.py:186
  1182.2 69.5 %collective-permute-done.5 = bf16[3072,512]{1,0:T(8,128)(2,1)S(1)} collective-permute-done((bf16[3072,512]{1,0:T(8,128)(2,1)S(1)}, bf16[3072,512]{1,0:T(8,128)(2,1)S(1)}, u32[]{:S(2)}, u32[]{:S(2)}) %collective-permute-start.5) | collective-permute-done | bytes 3145760 | tf_op jit(solution)/shard_map/ppermute | solution.py:186
  1251.7 21.1 %convert_reduce_fusion.5 = (f32[512]{0:T(512)S(1)}, bf16[6144,512]{1,0:T(8,128)(2,1)}) fusion(f32[6144,512]{1,0:T(8,128)} %get-tuple-element.115, f32[6144,512]{1,0:T(8,128)} %get-tuple-element.153, f32[512]{0:T(512)S(1)} %bitcast.503, bf16[1,512,512]{1,2,0:T(8,128)(2,1)S(1)} %copy-done.66, bf16[3072,512]{1,0:T(8,128)(2,1)S(1)} %collective-permute-done.5, ...), kind=kOutput, calls=%fused_computation.11 | convolution fusion | flops 3303013888 | bytes 38277120 | tf_op jit(solution)/shard_map/td,fd->tf/dot_general | solution.py:300
  1272.9 8.5 convolution_convert_fusion
  1282.1 70.4 %reduce-scatter.27.cloned.1.call-done = bf16[1536,512]{1,0:T(8,128)(2,1)} async-done(((bf16[6144,512]{1,0:T(8,128)(2,1)}), bf16[1536,512]{1,0:T(8,128)(2,1)}) %reduce-scatter.27.cloned.1.call-update) | async-done | bytes 1572880 | tf_op jit(solution)/shard_map/reduce_scatter | solution.py:208
  1362.5 7.8 fusion.149
  1373.9 5.9 fusion.161
  1380.7 30.2 %collective-permute-done.6 = bf16[1536,512]{1,0:T(8,128)(2,1)} collective-permute-done((bf16[1536,512]{1,0:T(8,128)(2,1)}, bf16[1536,512]{1,0:T(8,128)(2,1)}, u32[]{:S(2)}, u32[]{:S(2)}) %collective-permute-start.6) | collective-permute-done | bytes 1572896 | tf_op jit(solution)/shard_map/ppermute | solution.py:186
  1416.2 7.1 fusion.148
  1433.1 8.8 fusion.147
  1443.1 8.9 fusion.146
  1452.0 33.8 %collective-permute-done.7 = bf16[3072,512]{1,0:T(8,128)(2,1)} collective-permute-done((bf16[3072,512]{1,0:T(8,128)(2,1)}, bf16[3072,512]{1,0:T(8,128)(2,1)}, u32[]{:S(2)}, u32[]{:S(2)}) %collective-permute-start.7) | collective-permute-done | bytes 3145760 | tf_op jit(solution)/shard_map/ppermute | solution.py:186
  1485.9 7.5 convolution_convert_fusion.4
  1517.5 6.6 multiply_convert_fusion.2
  1543.5 10.2 copy.417
  1553.7 5.8 all-to-all-start.3
  1559.6 6.0 fusion.160
  1566.5 7.7 fusion.150
  1577.4 7.7 fusion.155
  1587.1 12.7 all-reduce.1
  1601.4 23.7 %reduce-scatter.31.cloned.1.call-done = bf16[1,3,64,128]{3,2,1,0:T(8,128)(2,1)} async-done(((bf16[1,3,512,128]{3,2,1,0:T(8,128)(2,1)}), bf16[1,3,64,128]{3,2,1,0:T(8,128)(2,1)}) %reduce-scatter.31.cloned.1.call-update) | async-done | bytes 49168 | tf_op jit(solution)/shard_map/reduce_scatter | solution.py:144
  1625.1 31.0 %reduce-scatter.29.cloned.1.call-done = bf16[1,3,64,128]{3,2,1,0:T(8,128)(2,1)} async-done(((bf16[1,3,512,128]{3,2,1,0:T(8,128)(2,1)}), bf16[1,3,64,128]{3,2,1,0:T(8,128)(2,1)}) %reduce-scatter.29.cloned.1.call-update) | async-done | bytes 49168 | tf_op jit(solution)/shard_map/reduce_scatter | solution.py:144
  1671.7 44.4 %all-reduce = (f32[2,2,512]{2,1,0:T(2,128)}, f32[2,2,512]{2,1,0:T(2,128)}, f32[2,2,512]{2,1,0:T(2,128)}) all-reduce(f32[2,2,512]{2,1,0:T(2,128)S(1)} %pad_maximum_fusion, f32[2,2,512]{2,1,0:T(2,128)S(1)} %pad_maximum_fusion.1, f32[2,2,512]{2,1,0:T(2,128)S(1)} %pad_maximum_fusion.2), channel_id=1, replica_groups=mesh['dp'=8,'tensor'=4] {'dp','tensor'}, use_global_device_ids=true, to_apply=%region_52.53 | all-reduce | flops 6144 | bytes 49152 | tf_op jit(solution)/shard_map/psum | solution.py:381
  (553 shorter events, 291.7 us)
Async XLA Ops:
  7.2 79.1 %all-gather.11.cloned.1.call-start = ((), (), s32[]{:S(2)}) async-start(), calls=%async_computation.16 | async-start | bytes 7864320 | tf_op jit(solution)/shard_map/all_gather | solution.py:170
  12.5 155.4 %copy-start.104 = (f32[1,1,512]{2,1,0:T(1,128)}, f32[1,1,512]{2,1,0:T(1,128)S(1)}, u32[]{:S(2)}) copy-start(f32[1,1,512]{2,1,0:T(1,128)S(1)} %get-tuple-element.140) | copy-start | bytes 6148
  15.7 95.9 %copy-start.126 = (pred[16,16]{1,0:T(8,128)(4,1)}, pred[16,16]{1,0:T(8,128)(4,1)S(1)}, u32[]{:S(2)}) copy-start(pred[16,16]{1,0:T(8,128)(4,1)S(1)} %iota_compare_fusion.1) | copy-start | bytes 772
  31.0 60.8 %copy-start.48 = (bf16[1,3,512,128]{3,2,1,0:T(8,128)(2,1)}, bf16[1,3,512,128]{3,2,1,0:T(8,128)(2,1)S(1)}, u32[]{:S(2)}) copy-start(bf16[1,3,512,128]{3,2,1,0:T(8,128)(2,1)S(1)} %all_gather.59) | copy-start | bytes 1179652
  131.5 30.4 %copy-start.123 = (f32[2,2,512]{2,1,0:T(2,128)S(1)}, f32[2,2,512]{2,1,0:T(2,128)}, u32[]{:S(2)}) copy-start(f32[2,2,512]{2,1,0:T(2,128)} %param.20) | copy-start | bytes 24580
  131.5 31.0 %all-to-all-start = ((bf16[4,1536,128]{2,1,0:T(8,128)(2,1)}), bf16[4,1536,128]{2,1,0:T(8,128)(2,1)S(1)}, u32[]{:S(2)}, u32[]{:S(2)}) async-start(bf16[4,1536,128]{2,1,0:T(8,128)(2,1)} %reshape.482), calls=%async_computation | async-start | bytes 3145728 | tf_op jit(solution)/shard_map/all_to_all | solution.py:252
  135.7 104.2 %all-gather.13.cloned.1.call-start = ((), (), s32[]{:S(2)}) async-start(), calls=%async_computation.17 | async-start | bytes 7864320 | tf_op jit(solution)/shard_map/all_gather | solution.py:170
  166.3 185.4 %copy-start = (f32[1536,512]{1,0:T(8,128)}, f32[1536,512]{1,0:T(8,128)S(1)}, u32[]{:S(2)}) copy-start(f32[1536,512]{1,0:T(8,128)S(1)} %get-tuple-element.117) | copy-start | bytes 9437188
  169.7 182.0 %reduce-scatter.21.cloned.1.call-start = ((), (), s32[]{:S(2)}) async-start(), calls=%async_computation.18 | async-start | bytes 7864320 | tf_op jit(solution)/shard_map/reduce_scatter | solution.py:199
  170.3 102.9 %copy-start.129 = (f32[1,512]{1,0:T(1,128)}, f32[1,512]{1,0:T(1,128)S(1)}, u32[]{:S(2)}) copy-start(f32[1,512]{1,0:T(1,128)S(1)} %get-tuple-element.148) | copy-start | bytes 6148
  239.9 36.1 %copy-start.65 = (bf16[1,512,512]{1,2,0:T(8,128)(2,1)S(1)}, bf16[1,512,512]{1,2,0:T(8,128)(2,1)}, u32[]{:S(2)}) copy-start(bf16[1,512,512]{1,2,0:T(8,128)(2,1)} %all_gather.64) | copy-start | bytes 1572868
  281.4 146.0 %all-gather.15.cloned.1.call-start = ((), (), s32[]{:S(2)}) async-start(), calls=%async_computation.19 | async-start | bytes 7864320 | tf_op jit(solution)/shard_map/all_gather | solution.py:170
  371.9 61.1 %copy-start.49 = (bf16[1,3,512,128]{3,2,1,0:T(8,128)(2,1)}, bf16[1,3,512,128]{3,2,1,0:T(8,128)(2,1)S(1)}, u32[]{:S(2)}) copy-start(bf16[1,3,512,128]{3,2,1,0:T(8,128)(2,1)S(1)} %all_gather.66) | copy-start | bytes 1179652
  472.7 33.1 %all-to-all-start.1 = ((bf16[4,1536,128]{2,1,0:T(8,128)(2,1)}), bf16[4,1536,128]{2,1,0:T(8,128)(2,1)}, u32[]{:S(2)}, u32[]{:S(2)}) async-start(bf16[4,1536,128]{2,1,0:T(8,128)(2,1)} %reshape.483), calls=%async_computation.2 | async-start | bytes 3145728 | tf_op jit(solution)/shard_map/all_to_all | solution.py:252
  477.5 146.4 %all-gather.17.cloned.1.call-start = ((), (), s32[]{:S(2)}) async-start(), calls=%async_computation.20 | async-start | bytes 7864320 | tf_op jit(solution)/shard_map/all_gather | solution.py:170
  513.3 274.7 %reduce-scatter.25.cloned.1.call-start = ((), (), s32[]{:S(2)}) async-start(), calls=%async_computation.22 | async-start | bytes 7864320 | tf_op jit(solution)/shard_map/reduce_scatter | solution.py:208
  516.1 55.9 %collective-permute-start = (bf16[1536,512]{1,0:T(8,128)(2,1)}, bf16[1536,512]{1,0:T(8,128)(2,1)}, u32[]{:S(2)}, u32[]{:S(2)}) collective-permute-start(bf16[1536,512]{1,0:T(8,128)(2,1)} %get-tuple-element.125), channel_id=1, source_target_pairs={{0,1},{1,0},{2,3},{3,2},{4,5},{5,4},{6,7},{7,6},{8,9},{9,8},{10,11... | collective-permute-start | bytes 4718600 | tf_op jit(solution)/shard_map/ppermute | solution.py:186
  517.4 60.5 %copy-start.78 = (bf16[1,512,64]{1,2,0:T(8,128)(2,1)S(1)}, bf16[1,512,64]{1,2,0:T(8,128)(2,1)}, u32[]{:S(2)}) copy-start(bf16[1,512,64]{1,2,0:T(8,128)(2,1)} %get-tuple-element.129) | copy-start | bytes 196612
  517.4 76.2 %copy-start.77 = (bf16[1,64,512]{2,1,0:T(8,128)(2,1)S(1)}, bf16[1,64,512]{2,1,0:T(8,128)(2,1)}, u32[]{:S(2)}) copy-start(bf16[1,64,512]{2,1,0:T(8,128)(2,1)} %get-tuple-element.127) | copy-start | bytes 196612
  575.3 91.7 %copy-start.50 = (bf16[3072,512]{1,0:T(8,128)(2,1)}, bf16[3072,512]{1,0:T(8,128)(2,1)S(1)}, u32[]{:S(2)}) copy-start(bf16[3072,512]{1,0:T(8,128)(2,1)S(1)} %maximum_select_fusion.4) | copy-start | bytes 9437188
  575.3 91.7 %collective-permute-start.1 = (bf16[3072,512]{1,0:T(8,128)(2,1)S(1)}, bf16[3072,512]{1,0:T(8,128)(2,1)}, u32[]{:S(2)}, u32[]{:S(2)}) collective-permute-start(bf16[3072,512]{1,0:T(8,128)(2,1)S(1)} %maximum_select_fusion.4), channel_id=1, source_target_pairs={{0,2},{1,3},{2,0},{3,1},{4,6},{5,7},{6,4},{7,5},{8,10},{9,11},{10,... | collective-permute-start | bytes 9437192 | tf_op jit(solution)/shard_map/ppermute | solution.py:186
  609.5 57.6 %copy-start.110 = (f32[1,512]{1,0:T(1,128)S(1)}, f32[1,512]{1,0:T(1,128)}, u32[]{:S(2)}) copy-start(f32[1,512]{1,0:T(1,128)} %get-tuple-element.147) | copy-start | bytes 6148
  624.0 43.0 %copy-start.67 = (bf16[1,512,512]{1,2,0:T(8,128)(2,1)S(1)}, bf16[1,512,512]{1,2,0:T(8,128)(2,1)}, u32[]{:S(2)}) copy-start(bf16[1,512,512]{1,2,0:T(8,128)(2,1)} %all_gather.71) | copy-start | bytes 1572868
  629.8 79.2 %copy-start.11 = (f32[6144,512]{1,0:T(8,128)}, f32[6144,512]{1,0:T(8,128)S(1)}, u32[]{:S(2)}) copy-start(f32[6144,512]{1,0:T(8,128)S(1)} %fusion.211) | copy-start | bytes 37748740
  667.0 44.5 %copy-start.55 = (bf16[1,512,512]{2,1,0:T(8,128)(2,1)S(1)}, bf16[1,512,512]{2,1,0:T(8,128)(2,1)}, u32[]{:S(2)}) copy-start(bf16[1,512,512]{2,1,0:T(8,128)(2,1)} %all_gather.70) | copy-start | bytes 1572868
  716.9 144.3 %reduce-scatter.23.cloned.1.call-start = ((), (), s32[]{:S(2)}) async-start(), calls=%async_computation.21 | async-start | bytes 7864320 | tf_op jit(solution)/shard_map/reduce_scatter | solution.py:199
  735.4 52.6 %copy-start.6 = (f32[1536,512]{1,0:T(8,128)S(1)}, f32[1536,512]{1,0:T(8,128)}, u32[]{:S(2)}) copy-start(f32[1536,512]{1,0:T(8,128)} %copy-done.5) | copy-start | bytes 9437188
  791.2 70.0 %copy-start.118 = (f32[1,1,512]{2,1,0:T(1,128)S(1)}, f32[1,1,512]{2,1,0:T(1,128)}, u32[]{:S(2)}) copy-start(f32[1,1,512]{2,1,0:T(1,128)} %get-tuple-element.135) | copy-start | bytes 6148
  866.3 37.4 %copy-start.14 = (f32[1536,512]{1,0:T(8,128)}, f32[1536,512]{1,0:T(8,128)S(1)}, u32[]{:S(2)}) copy-start(f32[1536,512]{1,0:T(8,128)S(1)} %get-tuple-element.101) | copy-start | bytes 9437188
  866.5 38.0 %copy-start.59 = (f32[3,16,2,128]{3,1,2,0:T(8,128)S(1)}, f32[3,16,2,128]{3,1,2,0:T(8,128)}, u32[]{:S(2)}) copy-start(f32[3,16,2,128]{3,1,2,0:T(8,128)} %get-tuple-element.106) | copy-start | bytes 147460
  866.5 107.9 %copy-start.63 = (bf16[1,128,512]{1,2,0:T(8,128)(2,1)S(1)}, bf16[1,128,512]{1,2,0:T(8,128)(2,1)}, u32[]{:S(2)}) copy-start(bf16[1,128,512]{1,2,0:T(8,128)(2,1)} %copy-done.62) | copy-start | bytes 393220
  866.5 36.2 %collective-permute-start.2 = (bf16[1536,512]{1,0:T(8,128)(2,1)S(1)}, bf16[1536,512]{1,0:T(8,128)(2,1)S(1)}, u32[]{:S(2)}, u32[]{:S(2)}) collective-permute-start(bf16[1536,512]{1,0:T(8,128)(2,1)S(1)} %convert_element_type.442), channel_id=1, source_target_pairs={{0,1},{1,0},{2,3},{3,2},{4,5},{5,4},{6,7},{7,6},{8,9},{9,8},{10,11... | collective-permute-start | bytes 4718600 | tf_op jit(solution)/shard_map/ppermute | solution.py:186
  903.7 69.1 %copy-start.52 = (bf16[3072,512]{1,0:T(8,128)(2,1)}, bf16[3072,512]{1,0:T(8,128)(2,1)S(1)}, u32[]{:S(2)}) copy-start(bf16[3072,512]{1,0:T(8,128)(2,1)S(1)} %maximum_select_fusion.5) | copy-start | bytes 9437188
  903.7 69.0 %collective-permute-start.3 = (bf16[3072,512]{1,0:T(8,128)(2,1)S(1)}, bf16[3072,512]{1,0:T(8,128)(2,1)S(1)}, u32[]{:S(2)}, u32[]{:S(2)}) collective-permute-start(bf16[3072,512]{1,0:T(8,128)(2,1)S(1)} %maximum_select_fusion.5), channel_id=1, source_target_pairs={{0,2},{1,3},{2,0},{3,1},{4,6},{5,7},{6,4},{7,5},{8,10},{9,11},{10,... | collective-permute-start | bytes 9437192 | tf_op jit(solution)/shard_map/ppermute | solution.py:186
  1043.3 86.4 %all-to-all-start.2 = ((bf16[6144,3,128]{2,1,0:T(4,128)(2,1)}), bf16[6144,3,128]{2,1,0:T(4,128)(2,1)}, u32[]{:S(2)}, u32[]{:S(2)}) async-start(bf16[6144,3,128]{2,1,0:T(4,128)(2,1)} %copy.393), calls=%async_computation.5 | async-start | bytes 12582912 | tf_op jit(solution)/shard_map/all_to_all | solution.py:330
  1049.1 67.4 %all-gather.19.cloned.1.call-start = ((), (), s32[]{:S(2)}) async-start(), calls=%async_computation.28 | async-start | bytes 1966080 | tf_op jit(solution)/shard_map/all_gather | solution.py:249
  1049.9 302.6 %reduce-scatter.27.cloned.1.call-start = ((), (), s32[]{:S(2)}) async-start(), calls=%async_computation.23 | async-start | bytes 7864320 | tf_op jit(solution)/shard_map/reduce_scatter | solution.py:208
  1143.2 38.9 %copy-start.16 = (f32[1536,512]{1,0:T(8,128)}, f32[1536,512]{1,0:T(8,128)S(1)}, u32[]{:S(2)}) copy-start(f32[1536,512]{1,0:T(8,128)S(1)} %get-tuple-element.99) | copy-start | bytes 9437188
  1143.4 108.3 %copy-start.66 = (bf16[1,512,512]{1,2,0:T(8,128)(2,1)S(1)}, bf16[1,512,512]{1,2,0:T(8,128)(2,1)}, u32[]{:S(2)}) copy-start(bf16[1,512,512]{1,2,0:T(8,128)(2,1)} %all_gather.64) | copy-start | bytes 1572868
  1143.4 108.3 %copy-start.130 = (f32[1,512]{1,0:T(1,128)S(1)}, f32[1,512]{1,0:T(1,128)}, u32[]{:S(2)}) copy-start(f32[1,512]{1,0:T(1,128)} %copy-done.129) | copy-start | bytes 6148
  1143.4 37.7 %collective-permute-start.4 = (bf16[1536,512]{1,0:T(8,128)(2,1)S(1)}, bf16[1536,512]{1,0:T(8,128)(2,1)S(1)}, u32[]{:S(2)}, u32[]{:S(2)}) collective-permute-start(bf16[1536,512]{1,0:T(8,128)(2,1)S(1)} %convert_element_type.456), channel_id=1, source_target_pairs={{0,1},{1,0},{2,3},{3,2},{4,5},{5,4},{6,7},{7,6},{8,9},{9,8},{10,11... | collective-permute-start | bytes 4718600 | tf_op jit(solution)/shard_map/ppermute | solution.py:186
  1182.1 90.8 %copy-start.53 = (bf16[3072,512]{1,0:T(8,128)(2,1)}, bf16[3072,512]{1,0:T(8,128)(2,1)S(1)}, u32[]{:S(2)}) copy-start(bf16[3072,512]{1,0:T(8,128)(2,1)S(1)} %maximum_select_fusion.6) | copy-start | bytes 9437188
  1182.1 69.6 %collective-permute-start.5 = (bf16[3072,512]{1,0:T(8,128)(2,1)S(1)}, bf16[3072,512]{1,0:T(8,128)(2,1)S(1)}, u32[]{:S(2)}, u32[]{:S(2)}) collective-permute-start(bf16[3072,512]{1,0:T(8,128)(2,1)S(1)} %maximum_select_fusion.6), channel_id=1, source_target_pairs={{0,2},{1,3},{2,0},{3,1},{4,6},{5,7},{6,4},{7,5},{8,10},{9,11},{10,... | collective-permute-start | bytes 9437192 | tf_op jit(solution)/shard_map/ppermute | solution.py:186
  1251.7 21.2 %copy-start.137 = (bf16[3072,512]{1,0:T(8,128)(2,1)}, bf16[3072,512]{1,0:T(8,128)(2,1)S(1)}, u32[]{:S(2)}) copy-start(bf16[3072,512]{1,0:T(8,128)(2,1)S(1)} %collective-permute-done.5) | copy-start | bytes 9437188
  1281.4 71.1 %copy-start.1 = (f32[1536,512]{1,0:T(8,128)S(1)}, f32[1536,512]{1,0:T(8,128)}, u32[]{:S(2)}) copy-start(f32[1536,512]{1,0:T(8,128)} %copy-done) | copy-start | bytes 9437188
  1281.4 71.1 %copy-start.76 = (f32[1536]{0:T(1024)S(1)}, f32[1536]{0:T(1024)}, u32[]{:S(2)}) copy-start(f32[1536]{0:T(1024)} %copy-done.75) | copy-start | bytes 18436
  1281.4 71.1 %copy-start.105 = (f32[1,1,512]{2,1,0:T(1,128)S(1)}, f32[1,1,512]{2,1,0:T(1,128)}, u32[]{:S(2)}) copy-start(f32[1,1,512]{2,1,0:T(1,128)} %copy-done.104) | copy-start | bytes 6148
  1281.4 73.8 %copy-start.98 = (f32[1536]{0:T(1024)S(1)}, f32[1536]{0:T(1024)}, u32[]{:S(2)}) copy-start(f32[1536]{0:T(1024)} %copy-done.97) | copy-start | bytes 18436
  1281.4 73.8 %copy-start.89 = (f32[1536]{0:T(1024)S(1)}, f32[1536]{0:T(1024)}, u32[]{:S(2)}) copy-start(f32[1536]{0:T(1024)} %copy-done.88) | copy-start | bytes 18436
  1281.4 145.4 %all-gather.21.cloned.1.call-start = ((), (), s32[]{:S(2)}) async-start(), calls=%async_computation.29 | async-start | bytes 1966080 | tf_op jit(solution)/shard_map/all_gather | solution.py:249
  1282.0 159.9 %reduce-scatter.43.cloned.1.call-start = ((), (), s32[]{:S(2)}) async-start(), calls=%async_computation.33 | async-start | bytes 589824
  1361.8 49.1 %collective-permute-start.6 = (bf16[1536,512]{1,0:T(8,128)(2,1)}, bf16[1536,512]{1,0:T(8,128)(2,1)}, u32[]{:S(2)}, u32[]{:S(2)}) collective-permute-start(bf16[1536,512]{1,0:T(8,128)(2,1)} %convert_element_type.460), channel_id=1, source_target_pairs={{0,1},{1,0},{2,3},{3,2},{4,5},{5,4},{6,7},{7,6},{8,9},{9,8},{10,11... | collective-permute-start | bytes 4718600 | tf_op jit(solution)/shard_map/ppermute | solution.py:186
  1372.1 202.3 %reduce-scatter.39.cloned.1.call-start = ((), (), s32[]{:S(2)}) async-start(), calls=%async_computation.31 | async-start | bytes 147456
  1380.7 35.6 %copy-start.54 = (bf16[3072,512]{1,0:T(8,128)(2,1)S(1)}, bf16[3072,512]{1,0:T(8,128)(2,1)}, u32[]{:S(2)}) copy-start(bf16[3072,512]{1,0:T(8,128)(2,1)} %copy-done.53) | copy-start | bytes 9437188
  1380.7 194.7 %reduce-scatter.41.cloned.1.call-start = ((), (), s32[]{:S(2)}) async-start(), calls=%async_computation.32 | async-start | bytes 589824
  1380.7 35.5 %copy-start.138 = (bf16[3072,512]{1,0:T(8,128)(2,1)S(1)}, bf16[3072,512]{1,0:T(8,128)(2,1)}, u32[]{:S(2)}) copy-start(bf16[3072,512]{1,0:T(8,128)(2,1)} %copy-done.137) | copy-start | bytes 9437188
  1415.7 70.2 %collective-permute-start.7 = (bf16[3072,512]{1,0:T(8,128)(2,1)}, bf16[3072,512]{1,0:T(8,128)(2,1)}, u32[]{:S(2)}, u32[]{:S(2)}) collective-permute-start(bf16[3072,512]{1,0:T(8,128)(2,1)} %maximum_select_fusion.7), channel_id=1, source_target_pairs={{0,2},{1,3},{2,0},{3,1},{4,6},{5,7},{6,4},{7,5},{8,10},{9,11},{10,... | collective-permute-start | bytes 9437192 | tf_op jit(solution)/shard_map/ppermute | solution.py:186
  1426.8 158.4 %reduce-scatter.35.cloned.1.call-start = ((), (), s32[]{:S(2)}) async-start(), calls=%async_computation.27 | async-start | bytes 589824 | tf_op jit(solution)/shard_map/reduce_scatter | solution.py:150
  1441.9 143.3 %reduce-scatter.33.cloned.1.call-start = ((), (), s32[]{:S(2)}) async-start(), calls=%async_computation.26 | async-start | bytes 589824 | tf_op jit(solution)/shard_map/reduce_scatter | solution.py:150
  1443.1 42.8 %copy-start.61 = (bf16[1,128,512]{1,2,0:T(8,128)(2,1)S(1)}, bf16[1,128,512]{1,2,0:T(8,128)(2,1)}, u32[]{:S(2)}) copy-start(bf16[1,128,512]{1,2,0:T(8,128)(2,1)} %copy-done.60) | copy-start | bytes 393220
  1553.7 103.8 %all-to-all-start.3 = ((bf16[6144,3,128]{2,1,0:T(4,128)(2,1)}), bf16[6144,3,128]{2,1,0:T(4,128)(2,1)}, u32[]{:S(2)}, u32[]{:S(2)}) async-start(bf16[6144,3,128]{2,1,0:T(4,128)(2,1)} %copy.417), calls=%async_computation.7 | async-start | bytes 12582912 | tf_op jit(solution)/shard_map/all_to_all | solution.py:330
  1559.6 40.2 %reduce-scatter.37.cloned.1.call-start = ((), (), s32[]{:S(2)}) async-start(), calls=%async_computation.30 | async-start | bytes 147456
  1566.5 58.6 %reduce-scatter.31.cloned.1.call-start = ((), (), s32[]{:S(2)}) async-start(), calls=%async_computation.25 | async-start | bytes 442368 | tf_op jit(solution)/shard_map/reduce_scatter | solution.py:144
  1574.4 81.7 %reduce-scatter.29.cloned.1.call-start = ((), (), s32[]{:S(2)}) async-start(), calls=%async_computation.24 | async-start | bytes 442368 | tf_op jit(solution)/shard_map/reduce_scatter | solution.py:144
  (111 other events, 495.5 us)
Sparse Core Ops, SparseCore 0:
  15.0 71.2 all-gather.10
  169.8 70.1 all-gather.12
  281.6 70.0 reduce-scatter.20
  357.1 70.3 all-gather.14
  513.4 110.5 all-gather.16
  717.0 70.9 reduce-scatter.24
  791.0 70.1 reduce-scatter.22
  1051.8 64.6 all-gather.18
  1281.5 70.9 reduce-scatter.26
  1354.2 43.3 all-gather.20
  1399.8 27.3 reduce-scatter.42
  1429.9 28.2 reduce-scatter.38
  1460.5 29.0 reduce-scatter.40
  1491.8 29.1 reduce-scatter.34
  1523.1 29.0 reduce-scatter.32
  1566.5 27.5 reduce-scatter.36
  1596.3 28.7 reduce-scatter.30
  1627.3 28.7 reduce-scatter.28
